TPU v7x, 32 devices: a whole 2x2x4 slice. The times are simulated.
32 devices in a mesh: pole: 2 (over y), row: 4 (over x, core), col: 4 (over z).
Axes of the slice: x: 2, y: 2, z: 4, core: 2. Of those that a mesh axis runs over, the one named last changes fastest.
Arguments:
- inverse_blocks: float32 [4096, 2048], P(('pole', 'row'), 'col'), parts along dimension 0, may hold values from -6 to 6
- lower_panel: float32 [4096, 512], P(('pole', 'row'), 'col'), parts along dimension 0, may hold values from -0.125 to 0.125
- struct_mask: int32 [16, 4], P('row', 'col'), may hold values 0 or 1
- diag_inverse: float32 [1024, 128], P(('pole', 'col')), parts along dimension 0, may hold values from -6 to 6
Outputs:
- g_panel: float32 [4096, 512], P(('pole', 'row'), 'col'), parts along dimension 0
- g_diag: float32 [1024, 128], P(('pole', 'col')), parts along dimension 0
There are 2 independent parts, one for each index of `pole`. A program takes and returns all parts, laid end to end along the dimension named above; an argument that names none is the same for every part. Nothing has to cross between parts.
All inputs are finite; a program needn't handle non-finite values. No bound on the sum of `struct_mask` on one device may be relied on, other than what follows from the above.
Results may differ from a plain program's by a relative error of at most 0.000071.
Values sent between devices are 32-bit elements; how exact they have to be, the bound alone decides.
No kernel may reach another device: no remote copies, remote signals or barrier semaphores. Data moves between devices by JAX's collectives and lax.ppermute only.
A program may use at most 64 MiB of HBM per device.

v0:
```python
import jax
import jax.numpy as jnp
from jax import lax
from jax.sharding import PartitionSpec as P


def from_root(x, axis, root):
    mine = lax.axis_index(axis) == root
    return lax.psum(jnp.where(mine, x, jnp.zeros_like(x)), axis)


def on_device(inverse_blocks, lower_panel, struct_mask, diag_inverse):
    width = diag_inverse.shape[1]
    local_rows = lower_panel.shape[0]
    local_cols = lower_panel.shape[1]
    supers = local_cols // width
    expanded = jnp.repeat(jnp.repeat(struct_mask, width, axis=0), width, axis=1).astype(jnp.float32)
    masked = lower_panel * expanded
    panel_row = lax.all_gather(masked, "col", axis=1, tiled=True)
    mirrored = from_root(panel_row, "row", lax.axis_index("col"))
    summed = lax.psum_scatter(
        lax.dot_general(
            mirrored,
            inverse_blocks,
            (((0,), (1,)), ((), ())),
            precision=lax.Precision.HIGHEST,
            preferred_element_type=jnp.float32,
        ),
        "col",
        scatter_dimension=0,
        tiled=True,
    )
    g_panel = -summed.T * expanded
    masked_three = masked.reshape(local_rows, supers, width)
    panel_three = g_panel.reshape(local_rows, supers, width)
    quad_part = -jnp.einsum(
        "jka,jkb->kab", masked_three, panel_three, precision=lax.Precision.HIGHEST
    )
    quad_total = lax.psum(quad_part, "row")
    g_diag = diag_inverse + quad_total.reshape(supers * width, width)
    return (g_panel, g_diag)


def solution(mesh):
    placed = (
        P(("pole", "row"), "col"),
        P(("pole", "row"), "col"),
        P("row", "col"),
        P(("pole", "col"), None),
    )
    return jax.shard_map(
        on_device,
        mesh=mesh,
        in_specs=placed,
        out_specs=(P(("pole", "row"), "col"), P(("pole", "col"), None)),
        check_vma=False,
    )
```

profile of v0, /device:TPU:0, one launch (start us, length us, event | category | flops | bytes accessed | tf_op | source)
XLA Modules:
  0.0 153.8 jit_solution(16746672606810595600)
XLA Ops:
  7.2 0.0 copy-start
  7.2 0.0 all-gather.2.cloned.1.call-start
  7.2 0.7 convert_bitcast_fusion
  8.0 0.1 broadcast_bitcast_fusion
  8.0 1.8 %broadcast_multiply_fusion = f32[512,128]{1,0:T(8,128)} fusion(f32[512,128]{1,0:T(8,128)} %param.5, f32[512]{0:T(512)S(1)} %broadcast_bitcast_fusion), kind=kLoop, calls=%fused_computation.5 | loop fusion | flops 65536 | bytes 526336 | tf_op jit(solution)/shard_map/mul | solution.py:18
  9.8 0.0 all-gather.2.cloned.1.call-update
  9.8 0.0 all-reduce.3.cloned.1.call-start
  9.9 33.2 %all-gather.2.cloned.1.call-done = f32[512,512]{1,0:T(8,128)} async-done(((f32[512,128]{1,0:T(8,128)}), f32[512,512]{1,0:T(8,128)}) %all-gather.2.cloned.1.call-update) | async-done | bytes 1048592 | tf_op jit(solution)/shard_map/all_gather | solution.py:19
  43.1 2.3 %broadcast_select_fusion = f32[512,512]{1,0:T(8,128)} fusion(f32[512,512]{1,0:T(8,128)} %all-gather.2.cloned.1.call-done, pred[]{:T(512)S(6)} %eq.3), kind=kLoop, calls=%fused_computation.1 | loop fusion | flops 262144 | bytes 2097153 | tf_op jit(solution)/shard_map/jit(_where)/select_n | solution.py:9
  45.4 0.0 all-reduce.3.cloned.1.call-update
  45.4 0.0 reduce-scatter.2.cloned.1.call-start
  45.5 34.4 %all-reduce.3.cloned.1.call-done = f32[512,512]{1,0:T(8,128)} async-done(((f32[512,512]{1,0:T(8,128)}), f32[512,512]{1,0:T(8,128)}) %all-reduce.3.cloned.1.call-update) | async-done | bytes 1048592 | tf_op jit(solution)/shard_map/psum | solution.py:9
  79.9 0.0 copy-done
  79.9 5.7 %fusion.2 = f32[512,512]{1,0:T(8,128)} fusion(f32[512,512]{1,0:T(8,128)} %all-reduce.3.cloned.1.call-done, f32[512,512]{1,0:T(8,128)S(1)} %copy-done), kind=kOutput, calls=%fused_computation.8 | convolution fusion | flops 1610612736 | bytes 3145728 | tf_op jit(solution)/shard_map/dot_general | solution.py:22
  85.6 0.0 copy-start.1
  85.6 0.0 reduce-scatter.2.cloned.1.call-update
  85.7 0.0 all-reduce.5.cloned.1.call-start
  85.7 27.6 %reduce-scatter.2.cloned.1.call-done = f32[128,512]{1,0:T(8,128)} async-done(((f32[512,512]{1,0:T(8,128)}), f32[128,512]{1,0:T(8,128)}) %reduce-scatter.2.cloned.1.call-update) | async-done | bytes 262160 | tf_op jit(solution)/shard_map/reduce_scatter | solution.py:21
  113.3 0.0 copy-done.1
  113.4 0.0 copy-start.2
  113.4 2.3 %convolution_negate_fusion = f32[128,128]{1,0:T(8,128)} fusion(f32[128,512]{1,0:T(8,128)} %reduce-scatter.2.cloned.1.call-done, f32[512]{0:T(512)S(1)} %broadcast_bitcast_fusion, f32[512,128]{1,0:T(8,128)S(1)} %copy-done.1), kind=kOutput, calls=%fused_computation | convolution fusion | flops 100876288 | bytes 591872 | tf_op jit(solution)/shard_map/jka,jkb->kab/dot_general | solution.py:36
  115.7 0.0 all-reduce.5.cloned.1.call-update
  115.7 0.0 copy-done.2
  115.8 0.0 copy-start.3
  115.8 0.8 copy.6
  116.6 29.2 %all-reduce.5.cloned.1.call-done = f32[128,128]{1,0:T(8,128)} async-done(((f32[128,128]{1,0:T(8,128)}), f32[128,128]{1,0:T(8,128)}) %all-reduce.5.cloned.1.call-update) | async-done | bytes 65552 | tf_op jit(solution)/shard_map/psum | solution.py:39
  145.8 0.0 copy-done.3
  145.8 1.5 add.9
  (1 shorter events, 0.0 us)
Async XLA Ops:
  7.2 72.7 %copy-start = (f32[512,512]{1,0:T(8,128)S(1)}, f32[512,512]{1,0:T(8,128)}, u32[]{:S(2)}) copy-start(f32[512,512]{1,0:T(8,128)} %param.4) | copy-start | bytes 3145732
  7.2 35.9 %all-gather.2.cloned.1.call-start = ((), (), s32[]{:S(2)}) async-start(), calls=%async_computation.1 | async-start | bytes 1310720 | tf_op jit(solution)/shard_map/all_gather | solution.py:19
  9.8 70.1 %all-reduce.3.cloned.1.call-start = ((), (), s32[]{:S(2)}) async-start(), calls=%async_computation.2 | async-start | bytes 2097152 | tf_op jit(solution)/shard_map/psum | solution.py:9
  45.4 67.9 %reduce-scatter.2.cloned.1.call-start = ((), (), s32[]{:S(2)}) async-start(), calls=%async_computation.3 | async-start | bytes 1310720 | tf_op jit(solution)/shard_map/reduce_scatter | solution.py:21
  85.6 27.7 %copy-start.1 = (f32[512,128]{1,0:T(8,128)S(1)}, f32[512,128]{1,0:T(8,128)}, u32[]{:S(2)}) copy-start(f32[512,128]{1,0:T(8,128)} %param.5) | copy-start | bytes 786436
  85.7 60.2 %all-reduce.5.cloned.1.call-start = ((), (), s32[]{:S(2)}) async-start(), calls=%async_computation.4 | async-start | bytes 131072 | tf_op jit(solution)/shard_map/psum | solution.py:39
  113.4 2.4 %copy-start.2 = (f32[128,512]{1,0:T(8,128)S(1)}, f32[128,512]{1,0:T(8,128)}, u32[]{:S(2)}) copy-start(f32[128,512]{1,0:T(8,128)} %reduce-scatter.2.cloned.1.call-done) | copy-start | bytes 786436
  115.8 30.1 %copy-start.3 = (f32[128,128]{1,0:T(8,128)S(1)}, f32[128,128]{1,0:T(8,128)}, u32[]{:S(2)}) copy-start(f32[128,128]{1,0:T(8,128)} %param.7) | copy-start | bytes 196612
Sparse Core Ops, SparseCore 0:
  10.1 32.8 all-gather.1
  45.6 34.2 all-reduce.2
  85.8 27.5 reduce-scatter.1
  116.1 29.6 all-reduce.4
where the time goes:
time: 154 us
  waiting for transfers between devices  124 us (81%)
  between operations  13.8 us (9%)
  matrix products  8.07 us (5%)
  other arithmetic  6.37 us (4%)
    psum x1, waiting for transfers between devices, from_root(): return lax.psum(jnp.where(mine, x, jnp.zeros_like(x)), axis)  34.4 us
    all_gather x1, waiting for transfers between devices, on_device(): panel_row = lax.all_gather(masked, 'col', axis=1, tiled=True)  33.2 us
    psum x1, waiting for transfers between devices, on_device(): quad_total = lax.psum(quad_part, 'row')  29.2 us
    reduce_scatter x1, waiting for transfers between devices, on_device(): lax.psum_scatter(lax.dot_general(mirrored, inverse_blocks, (((0,), (1,)),...  27.6 us
    dot_general x1, matrix products, on_device(): lax.dot_general(mirrored, inverse_blocks, (((0,), (1,)), ((), ())), preci...  5.73 us
  transfers between devices with their start and end apart: 4, of which 4 were waited for; matrix products, arithmetic and copies ran while one was open for 1% of the time, Pallas kernels for 0%

commit v1 on v0

--- a/solution.py
+++ b/solution.py
@@ -16,7 +16,19 @@
     supers = local_cols // width
     expanded = jnp.repeat(jnp.repeat(struct_mask, width, axis=0), width, axis=1).astype(jnp.float32)
     masked = lower_panel * expanded
-    panel_row = lax.all_gather(masked, "col", axis=1, tiled=True)
+    page = masked
+    mixed_arr, spare, formed = (lax.axis_size("col"), lax.axis_index("col"), page.shape[1])
+    grid = [hop_no * mixed_arr if tick == 1 else hop_no for tick, hop_no in enumerate(page.shape)]
+    panel_row = lax.dynamic_update_slice_in_dim(
+        jnp.zeros(grid, page.dtype), page, spare * formed, axis=1
+    )
+    for idx in [*range(1, mixed_arr)]:
+        page = lax.ppermute(
+            page, "col", [(tick, (tick + 1) % mixed_arr) for tick in range(mixed_arr)]
+        )
+        panel_row = lax.dynamic_update_slice_in_dim(
+            panel_row, page, (spare - idx) % mixed_arr * formed, axis=1
+        )
     mirrored = from_root(panel_row, "row", lax.axis_index("col"))
     summed = lax.psum_scatter(
         lax.dot_general(

time: 154 us -> 148 us (0.961)
  waiting for transfers between devices: 124 us -> 117 us
  other arithmetic: 6.37 us -> 2.75 us
  starting transfers between devices: 0.16 us -> 3.2 us
  local copies, waits for them, and re-layouts: 0.93 us -> 2.68 us
    all_gather x1 -> x0, waiting for transfers between devices: 33.2 us -> none  [on_device(): panel_row = lax.all_gather(masked, 'col', axis=1, tiled=True)]
    ppermute x0 -> x3, waiting for transfers between devices: none -> 25.9 us  [on_device(): lax.ppermute(page, 'col', [(tick, (tick + 1) % mixed_arr) for tick in ran...]
    ppermute x0 -> x3, starting transfers between devices: none -> 3.08 us  [on_device(): lax.ppermute(page, 'col', [(tick, (tick + 1) % mixed_arr) for tick in ran...]
    mul x1 -> x0, other arithmetic: 1.79 us -> none  [on_device(): masked = lower_panel * expanded]
    unnamed x9 -> x11, local copies, waits for them, and re-layouts: 0.86 us -> 2.41 us
  transfers between devices with their start and end apart: 4 -> 6, of which waited for: 4 -> 6; matrix products, arithmetic and copies ran while one was open for 1% -> 1% of each run, Pallas kernels for 0% -> 0%
where the time goes in v1:
time: 148 us; the launch traced here: 147 us
  waiting for transfers between devices  117 us (79%)
  between operations  13.8 us (9%)
  matrix products  7.96 us (5%)
  starting transfers between devices  3.2 us (2%)
  other arithmetic  2.75 us (2%)
  local copies, waits for them, and re-layouts  2.68 us (2%)
    psum x1, waiting for transfers between devices, from_root(): return lax.psum(jnp.where(mine, x, jnp.zeros_like(x)), axis)  34 us
    psum x1, waiting for transfers between devices, on_device(): quad_total = lax.psum(quad_part, 'row')  29.5 us
    reduce_scatter x1, waiting for transfers between devices, on_device(): lax.psum_scatter(lax.dot_general(mirrored, inverse_blocks, (((0,), (1,)),...  27.6 us
    ppermute x3, waiting for transfers between devices, on_device(): lax.ppermute(page, 'col', [(tick, (tick + 1) % mixed_arr) for tick in ran...  25.9 us
    dot_general x1, matrix products, on_device(): lax.dot_general(mirrored, inverse_blocks, (((0,), (1,)), ((), ())), preci...  5.72 us
    ppermute x3, starting transfers between devices, on_device(): lax.ppermute(page, 'col', [(tick, (tick + 1) % mixed_arr) for tick in ran...  3.08 us
  transfers between devices with their start and end apart: 6, of which 6 were waited for; matrix products, arithmetic and copies ran while one was open for 1% of the time, Pallas kernels for 0%

profile of v1, /device:TPU:0, one launch (start us, length us, event | category | flops | bytes accessed | tf_op | source)
XLA Modules:
  0.0 147.5 jit_solution(8218560939800806073)
XLA Ops:
  7.2 0.0 copy-start
  7.2 0.0 all-reduce.3.cloned.1.call-start
  7.2 0.0 copy-start.4
  7.2 0.7 copy-done.4
  8.0 0.1 broadcast_bitcast_fusion
  8.0 0.0 copy-start.2
  8.0 0.1 broadcast.14
  8.2 0.8 copy-done.2
  9.0 0.1 constant_dynamic-update-slice_fusion.3
  9.1 3.1 %collective-permute-start = (f32[512,128]{1,0:T(8,128)S(1)}, f32[512,128]{1,0:T(8,128)S(1)}, u32[]{:S(2)}, u32[]{:S(2)}) collective-permute-start(f32[512,128]{1,0:T(8,128)S(1)} %get-tuple-element.5), channel_id=1, source_target_pairs={{0,1},{1,2},{2,3},{3,0},{4,5},{5,6},{6,7},{7,4},{8,9},{9,10},{10,1... | collective-permute-start | bytes 786440 | tf_op jit(solution)/shard_map/ppermute | solution.py:26
  12.2 8.3 %collective-permute-done = f32[512,128]{1,0:T(8,128)S(1)} collective-permute-done((f32[512,128]{1,0:T(8,128)S(1)}, f32[512,128]{1,0:T(8,128)S(1)}, u32[]{:S(2)}, u32[]{:S(2)}) %collective-permute-start) | collective-permute-done | bytes 262176 | tf_op jit(solution)/shard_map/ppermute | solution.py:26
  20.5 0.0 collective-permute-start.1
  20.5 9.3 %collective-permute-done.1 = f32[512,128]{1,0:T(8,128)S(1)} collective-permute-done((f32[512,128]{1,0:T(8,128)S(1)}, f32[512,128]{1,0:T(8,128)S(1)}, u32[]{:S(2)}, u32[]{:S(2)}) %collective-permute-start.1) | collective-permute-done | bytes 262176 | tf_op jit(solution)/shard_map/ppermute | solution.py:26
  29.8 0.0 collective-permute-start.2
  29.9 8.3 %collective-permute-done.2 = f32[512,128]{1,0:T(8,128)S(1)} collective-permute-done((f32[512,128]{1,0:T(8,128)S(1)}, f32[512,128]{1,0:T(8,128)S(1)}, u32[]{:S(2)}, u32[]{:S(2)}) %collective-permute-start.2) | collective-permute-done | bytes 262176 | tf_op jit(solution)/shard_map/ppermute | solution.py:26
  38.2 1.1 broadcast_select_fusion
  39.3 0.0 all-reduce.3.cloned.1.call-update
  39.4 0.0 reduce-scatter.2.cloned.1.call-start
  39.4 34.0 %all-reduce.3.cloned.1.call-done = f32[512,512]{1,0:T(8,128)} async-done(((f32[512,512]{1,0:T(8,128)}), f32[512,512]{1,0:T(8,128)}) %all-reduce.3.cloned.1.call-update) | async-done | bytes 1048592 | tf_op jit(solution)/shard_map/psum | solution.py:9
  73.4 0.0 copy-done
  73.4 5.7 %fusion.2 = f32[512,512]{1,0:T(8,128)} fusion(f32[512,512]{1,0:T(8,128)} %all-reduce.3.cloned.1.call-done, f32[512,512]{1,0:T(8,128)S(1)} %copy-done), kind=kOutput, calls=%fused_computation.12 | convolution fusion | flops 1610612736 | bytes 3145728 | tf_op jit(solution)/shard_map/dot_general | solution.py:34
  79.1 0.0 reduce-scatter.2.cloned.1.call-update
  79.1 0.0 all-reduce.5.cloned.1.call-start
  79.2 27.6 %reduce-scatter.2.cloned.1.call-done = f32[128,512]{1,0:T(8,128)} async-done(((f32[512,512]{1,0:T(8,128)}), f32[128,512]{1,0:T(8,128)}) %reduce-scatter.2.cloned.1.call-update) | async-done | bytes 262160 | tf_op jit(solution)/shard_map/reduce_scatter | solution.py:33
  106.8 0.0 copy-start.1
  106.8 2.2 %convolution_negate_fusion = f32[128,128]{1,0:T(8,128)} fusion(f32[512,128]{1,0:T(8,128)S(1)} %get-tuple-element.5, f32[128,512]{1,0:T(8,128)} %reduce-scatter.2.cloned.1.call-done, f32[512]{0:T(512)S(1)} %broadcast_bitcast_fusion), kind=kOutput, calls=%fused_computation | convolution fusion | flops 100810752 | bytes 591872 | tf_op jit(solution)/shard_map/jka,jkb->kab/dot_general | solution.py:48
  109.1 0.0 all-reduce.5.cloned.1.call-update
  109.1 0.0 copy-done.1
  109.1 0.0 copy-start.3
  109.2 0.8 copy.6
  110.0 29.5 %all-reduce.5.cloned.1.call-done = f32[128,128]{1,0:T(8,128)} async-done(((f32[128,128]{1,0:T(8,128)}), f32[128,128]{1,0:T(8,128)}) %all-reduce.5.cloned.1.call-update) | async-done | bytes 65552 | tf_op jit(solution)/shard_map/psum | solution.py:51
  139.5 0.0 copy-done.3
  139.5 1.5 %add.41 = f32[128,128]{1,0:T(8,128)} add(f32[128,128]{1,0:T(8,128)S(1)} %copy-done.3, f32[128,128]{1,0:T(8,128)} %all-reduce.5.cloned.1.call-done) | non-fusion elementwise | flops 16384 | bytes 196608 | tf_op jit(solution)/shard_map/add | solution.py:52
  (5 shorter events, 0.1 us)
Async XLA Ops:
  7.2 66.2 %copy-start = (f32[512,512]{1,0:T(8,128)S(1)}, f32[512,512]{1,0:T(8,128)}, u32[]{:S(2)}) copy-start(f32[512,512]{1,0:T(8,128)} %param.4) | copy-start | bytes 3145732
  7.2 66.2 %all-reduce.3.cloned.1.call-start = ((), (), s32[]{:S(2)}) async-start(), calls=%async_computation.1 | async-start | bytes 2097152 | tf_op jit(solution)/shard_map/psum | solution.py:9
  7.2 0.7 copy-start.4
  8.0 0.9 copy-start.2
  9.1 11.4 %collective-permute-start = (f32[512,128]{1,0:T(8,128)S(1)}, f32[512,128]{1,0:T(8,128)S(1)}, u32[]{:S(2)}, u32[]{:S(2)}) collective-permute-start(f32[512,128]{1,0:T(8,128)S(1)} %get-tuple-element.5), channel_id=1, source_target_pairs={{0,1},{1,2},{2,3},{3,0},{4,5},{5,6},{6,7},{7,4},{8,9},{9,10},{10,1... | collective-permute-start | bytes 786440 | tf_op jit(solution)/shard_map/ppermute | solution.py:26
  20.5 9.3 %collective-permute-start.1 = (f32[512,128]{1,0:T(8,128)S(1)}, f32[512,128]{1,0:T(8,128)S(1)}, u32[]{:S(2)}, u32[]{:S(2)}) collective-permute-start(f32[512,128]{1,0:T(8,128)S(1)} %collective-permute-done), channel_id=1, source_target_pairs={{0,1},{1,2},{2,3},{3,0},{4,5},{5,6},{6,7},{7,4},{8,9},{9,10},{10,1... | collective-permute-start | bytes 786440 | tf_op jit(solution)/shard_map/ppermute | solution.py:26
  29.8 8.4 %collective-permute-start.2 = (f32[512,128]{1,0:T(8,128)S(1)}, f32[512,128]{1,0:T(8,128)S(1)}, u32[]{:S(2)}, u32[]{:S(2)}) collective-permute-start(f32[512,128]{1,0:T(8,128)S(1)} %collective-permute-done.1), channel_id=1, source_target_pairs={{0,1},{1,2},{2,3},{3,0},{4,5},{5,6},{6,7},{7,4},{8,9},{9,10},{10,1... | collective-permute-start | bytes 786440 | tf_op jit(solution)/shard_map/ppermute | solution.py:26
  39.4 67.5 %reduce-scatter.2.cloned.1.call-start = ((), (), s32[]{:S(2)}) async-start(), calls=%async_computation.2 | async-start | bytes 1310720 | tf_op jit(solution)/shard_map/reduce_scatter | solution.py:33
  79.1 60.3 %all-reduce.5.cloned.1.call-start = ((), (), s32[]{:S(2)}) async-start(), calls=%async_computation.3 | async-start | bytes 131072 | tf_op jit(solution)/shard_map/psum | solution.py:51
  106.8 2.3 %copy-start.1 = (f32[128,512]{1,0:T(8,128)S(1)}, f32[128,512]{1,0:T(8,128)}, u32[]{:S(2)}) copy-start(f32[128,512]{1,0:T(8,128)} %reduce-scatter.2.cloned.1.call-done) | copy-start | bytes 786436
  109.1 30.3 %copy-start.3 = (f32[128,128]{1,0:T(8,128)S(1)}, f32[128,128]{1,0:T(8,128)}, u32[]{:S(2)}) copy-start(f32[128,128]{1,0:T(8,128)} %param.7) | copy-start | bytes 196612
Sparse Core Ops, SparseCore 0:
  39.5 33.8 all-reduce.2
  79.3 27.5 reduce-scatter.1
  109.7 29.6 all-reduce.4

commit v2 on v0

--- a/solution.py
+++ b/solution.py
@@ -36,7 +36,12 @@
     quad_part = -jnp.einsum(
         "jka,jkb->kab", masked_three, panel_three, precision=lax.Precision.HIGHEST
     )
-    quad_total = lax.psum(quad_part, "row")
+
+    def object_update(packet):
+        carry = lax.all_gather(packet, "row").sum(axis=0)
+        return carry
+
+    quad_total = object_update(quad_part)
     g_diag = diag_inverse + quad_total.reshape(supers * width, width)
     return (g_panel, g_diag)
 

time: 154 us -> 130 us (0.84)
  waiting for transfers between devices: 124 us -> 95.3 us
  blocking collectives: 0 us -> 5.79 us
  matrix products: 8.07 us -> 6.39 us
    psum x1 -> x0, waiting for transfers between devices: 29.2 us -> none  [on_device(): quad_total = lax.psum(quad_part, 'row')]
    all_gather x0 -> x1, blocking collectives: none -> 5.79 us  [object_update(): carry = lax.all_gather(packet, 'row').sum(axis=0)]
    dot_general x1, matrix products: 2.34 us -> 0.69 us  [on_device(): jnp.einsum('jka,jkb->kab', masked_three, panel_three, precision=lax.Preci...]
  transfers between devices with their start and end apart: 4 -> 3, of which waited for: 4 -> 3; matrix products, arithmetic and copies ran while one was open for 1% -> 0% of each run, Pallas kernels for 0% -> 0%
where the time goes in v2:
time: 130 us
  waiting for transfers between devices  95.3 us (73%)
  between operations  13.8 us (11%)
  other arithmetic  6.47 us (5%)
  matrix products  6.39 us (5%)
  blocking collectives  5.79 us (4%)
  local copies, waits for them, and re-layouts  1.92 us (1%)
    psum x1, waiting for transfers between devices, from_root(): return lax.psum(jnp.where(mine, x, jnp.zeros_like(x)), axis)  34.4 us
    all_gather x1, waiting for transfers between devices, on_device(): panel_row = lax.all_gather(masked, 'col', axis=1, tiled=True)  33.2 us
    reduce_scatter x1, waiting for transfers between devices, on_device(): lax.psum_scatter(lax.dot_general(mirrored, inverse_blocks, (((0,), (1,)),...  27.7 us
    all_gather x1, blocking collectives, object_update(): carry = lax.all_gather(packet, 'row').sum(axis=0)  5.79 us
    dot_general x1, matrix products, on_device(): lax.dot_general(mirrored, inverse_blocks, (((0,), (1,)), ((), ())), preci...  5.71 us
  transfers between devices with their start and end apart: 3, of which 3 were waited for; matrix products, arithmetic and copies ran while one was open for 0% of the time, Pallas kernels for 0%

profile of v2, /device:TPU:0, one launch (start us, length us, event | category | flops | bytes accessed | tf_op | source)
XLA Modules:
  0.0 129.8 jit_solution(16104490052188918264)
XLA Ops:
  7.2 0.0 copy-start
  7.2 0.0 all-gather.3.cloned.1.call-start
  7.2 0.7 convert_bitcast_fusion
  8.0 0.1 broadcast_bitcast_fusion
  8.0 1.8 %broadcast_multiply_fusion = f32[512,128]{1,0:T(8,128)} fusion(f32[512,128]{1,0:T(8,128)} %param.5, f32[512]{0:T(512)S(1)} %broadcast_bitcast_fusion), kind=kLoop, calls=%fused_computation.5 | loop fusion | flops 65536 | bytes 526336 | tf_op jit(solution)/shard_map/mul | solution.py:18
  9.8 0.0 all-gather.3.cloned.1.call-update
  9.8 0.0 all-reduce.2.cloned.1.call-start
  9.9 33.2 %all-gather.3.cloned.1.call-done = f32[512,512]{1,0:T(8,128)} async-done(((f32[512,128]{1,0:T(8,128)}), f32[512,512]{1,0:T(8,128)}) %all-gather.3.cloned.1.call-update) | async-done | bytes 1048592 | tf_op jit(solution)/shard_map/all_gather | solution.py:19
  43.1 2.3 %broadcast_select_fusion = f32[512,512]{1,0:T(8,128)} fusion(f32[512,512]{1,0:T(8,128)} %all-gather.3.cloned.1.call-done, pred[]{:T(512)S(6)} %eq.3), kind=kLoop, calls=%fused_computation.1 | loop fusion | flops 262144 | bytes 2097153 | tf_op jit(solution)/shard_map/jit(_where)/select_n | solution.py:9
  45.4 0.0 all-reduce.2.cloned.1.call-update
  45.4 0.0 reduce-scatter.2.cloned.1.call-start
  45.5 34.4 %all-reduce.2.cloned.1.call-done = f32[512,512]{1,0:T(8,128)} async-done(((f32[512,512]{1,0:T(8,128)}), f32[512,512]{1,0:T(8,128)}) %all-reduce.2.cloned.1.call-update) | async-done | bytes 1048592 | tf_op jit(solution)/shard_map/psum | solution.py:9
  79.8 0.0 copy-done
  79.9 5.7 %fusion.2 = f32[512,512]{1,0:T(8,128)} fusion(f32[512,512]{1,0:T(8,128)} %all-reduce.2.cloned.1.call-done, f32[512,512]{1,0:T(8,128)S(1)} %copy-done), kind=kOutput, calls=%fused_computation.8 | convolution fusion | flops 1610612736 | bytes 3145728 | tf_op jit(solution)/shard_map/dot_general | solution.py:22
  85.6 0.0 reduce-scatter.2.cloned.1.call-update
  85.6 27.7 %reduce-scatter.2.cloned.1.call-done = f32[128,512]{1,0:T(8,128)} async-done(((f32[512,512]{1,0:T(8,128)}), f32[128,512]{1,0:T(8,128)}) %reduce-scatter.2.cloned.1.call-update) | async-done | bytes 262160 | tf_op jit(solution)/shard_map/reduce_scatter | solution.py:21
  113.3 1.0 fusion
  114.2 0.0 copy-start.1
  114.3 0.0 copy-start.2
  114.3 0.8 copy.6
  115.1 0.1 copy-done.1
  115.2 0.1 copy-done.2
  115.3 0.7 convolution_negate_fusion
  116.0 5.8 %all-gather = f32[512,128]{1,0:T(8,128)S(1)} all-gather(f32[128,128]{1,0:T(8,128)S(1)} %convolution_negate_fusion), channel_id=2, replica_groups=mesh['pole'=2,'row'=4,'col'=4] {'row'}, dimensions={0}, use_global_device_ids=true | all-gather | bytes 327680 | tf_op jit(solution)/shard_map/all_gather | solution.py:41
  121.8 0.0 copy-start.3
  121.8 0.8 copy-done.3
  122.6 0.6 add.7
  (1 shorter events, 0.0 us)
Async XLA Ops:
  7.2 72.7 %copy-start = (f32[512,512]{1,0:T(8,128)S(1)}, f32[512,512]{1,0:T(8,128)}, u32[]{:S(2)}) copy-start(f32[512,512]{1,0:T(8,128)} %param.4) | copy-start | bytes 3145732
  7.2 35.9 %all-gather.3.cloned.1.call-start = ((), (), s32[]{:S(2)}) async-start(), calls=%async_computation.1 | async-start | bytes 1310720 | tf_op jit(solution)/shard_map/all_gather | solution.py:19
  9.8 70.0 %all-reduce.2.cloned.1.call-start = ((), (), s32[]{:S(2)}) async-start(), calls=%async_computation.2 | async-start | bytes 2097152 | tf_op jit(solution)/shard_map/psum | solution.py:9
  45.4 67.8 %reduce-scatter.2.cloned.1.call-start = ((), (), s32[]{:S(2)}) async-start(), calls=%async_computation.3 | async-start | bytes 1310720 | tf_op jit(solution)/shard_map/reduce_scatter | solution.py:21
  114.2 1.0 copy-start.1
  114.3 1.0 copy-start.2
  121.8 0.8 copy-start.3
Sparse Core Ops, SparseCore 0:
  10.1 32.8 all-gather.2
  45.5 34.2 all-reduce.1
  85.7 27.5 reduce-scatter.1
